TPU v7x, 32 devices: a whole 2x2x4 slice. The times are simulated.
32 devices in a mesh: layer: 4 (over x, core), lat: 8 (over z, y).
Axes of the slice: x: 2, y: 2, z: 4, core: 2. Of those that a mesh axis runs over, the one named last changes fastest.
Arguments:
- resid_in: bfloat16 [4, 4096, 256], P('layer', 'lat'), may hold values from -6 to 6
- resid_out: bfloat16 [4, 4096, 256], P('layer', 'lat'), may hold values from -80 to 80
- token_ids: int32 [256], replicated, may hold values from 0 to 128255, as said below
- active_mask: int32 [4, 6144, 256], P('layer', 'lat'), may hold values 0 or 1
- enc_weight: bfloat16 [4, 6144, 4096], P('layer', 'lat'), may hold values from -0.09375 to 0.09375
- enc_bias: bfloat16 [4, 6144], P('layer', 'lat'), may hold values from -3 to 3
- dec_weight: bfloat16 [4, 4, 6144, 4096], P('layer', None, 'lat'), may hold values from -0.078125 to 0.078125
- dec_bias: bfloat16 [4, 4096], P('layer', 'lat'), may hold values from -3 to 3
Outputs:
- enc_grad: bfloat16 [4, 6144, 4096], P('layer', 'lat')
- dec_grad: bfloat16 [4, 4, 6144, 4096], P('layer', None, 'lat')
- total_loss: float32 [], replicated
Inputs may be any that keep to these rules, and one draw needn't show every extreme that they name: `token_ids`: ids of the Llama 3 vocabulary; the begin-of-text id 128000 stands at position 0 and at scattered other positions.
All inputs are finite; a program needn't handle non-finite values. No bound on the sum of `active_mask` on one device may be relied on, other than what follows from the above.
Results may differ from a plain program's by a relative error of at most 0.007.
Values may be sent and summed in bfloat16 or wider, within the bound.
A program may use at most 128 MiB of HBM per device.

v0:
```python
import jax
import jax.numpy as jnp
from jax import lax
from jax.sharding import PartitionSpec as P

EPSILON = 1e-05


def on_device(
    resid_in, resid_out, token_ids, active_mask, enc_weight, enc_bias, dec_weight, dec_bias
):
    layer_count = lax.axis_size("layer")
    layer_here = lax.axis_index("layer")
    inputs_local = resid_in[0]
    weight_enc = enc_weight[0]
    lat_rows = weight_enc.shape[0]
    feature_count = weight_enc.shape[1]
    token_count = inputs_local.shape[1]
    whole_inputs = lax.all_gather(inputs_local, "lat", axis=0, tiled=True)
    preact = jnp.dot(weight_enc, whole_inputs, preferred_element_type=jnp.float32)
    preact = preact + enc_bias[0].astype(jnp.float32)[:, None]
    gating = active_mask[0].astype(jnp.float32)
    latents = (gating * preact).astype(jnp.bfloat16)
    source_ids = jnp.arange(layer_count)
    gathered = lax.all_gather(latents[None], "layer", axis=0, tiled=True)
    acts_stack = jnp.where(
        (source_ids <= layer_here)[:, None, None], gathered, jnp.zeros((), jnp.bfloat16)
    )
    stack_rows = acts_stack.reshape(layer_count * lat_rows, token_count)
    weight_rows = dec_weight[0].reshape(layer_count * lat_rows, feature_count)
    kept_tokens = (token_ids != 128000).astype(jnp.float32)
    total_cells = feature_count * token_count
    wanted = resid_out[0].astype(jnp.float32)
    recon = lax.psum_scatter(
        lax.dot_general(
            weight_rows, stack_rows, (((0,), (0,)), ((), ())), preferred_element_type=jnp.float32
        ),
        "lat",
        scatter_dimension=0,
        tiled=True,
    )
    recon = recon + dec_bias[0].astype(jnp.float32)[:, None]
    centered = wanted - jnp.mean(wanted, axis=1, keepdims=True)
    residual_err = kept_tokens[None, :] * (recon - wanted)
    squares_err, squares_tgt = lax.psum(
        (jnp.sum(residual_err * residual_err), jnp.sum(centered * centered)), "lat"
    )
    spread = squares_tgt / total_cells + EPSILON
    layer_loss = squares_err / (2.0 * spread * total_cells)
    total_loss = lax.psum(layer_loss, "layer")
    out_grad = (residual_err / spread).astype(jnp.bfloat16)
    full_grad = lax.all_gather(out_grad, "lat", axis=0, tiled=True)
    grad_rows = jnp.dot(weight_rows, full_grad, preferred_element_type=jnp.float32).reshape(
        layer_count, lat_rows, token_count
    )
    grad_rows = grad_rows * (source_ids <= layer_here).astype(jnp.float32)[:, None, None]
    dec_out = lax.dot_general(
        stack_rows, full_grad, (((1,), (1,)), ((), ())), preferred_element_type=jnp.float32
    )
    dec_out = dec_out.astype(jnp.bfloat16).reshape(1, layer_count, lat_rows, feature_count)
    latent_grad = lax.psum_scatter(grad_rows, "layer", scatter_dimension=0, tiled=True)[0]
    preact_grad = (gating * latent_grad).astype(jnp.bfloat16)
    enc_out = lax.dot_general(
        preact_grad, whole_inputs, (((1,), (1,)), ((), ())), preferred_element_type=jnp.float32
    )
    return (enc_out.astype(jnp.bfloat16)[None], dec_out, total_loss)


def solution(mesh):
    in_specs = (
        P("layer", "lat", None),
        P("layer", "lat", None),
        P(),
        P("layer", "lat", None),
        P("layer", "lat", None),
        P("layer", "lat"),
        P("layer", None, "lat", None),
        P("layer", "lat"),
    )
    out_specs = (P("layer", "lat", None), P("layer", None, "lat", None), P())
    return jax.shard_map(
        on_device, mesh=mesh, in_specs=in_specs, out_specs=out_specs, check_vma=False
    )
```

profile of v0, /device:TPU:0, one launch (start us, length us, event | category | flops | bytes accessed | tf_op | source)
XLA Modules:
  0.0 334.2 jit_solution(15536479008416231452)
XLA Ops:
  7.2 0.0 all-gather.8.cloned.1.call-start
  7.2 0.7 all-gather.8.cloned.1.call-update
  7.9 0.0 all-gather.10.cloned.1.call-start
  7.9 0.7 convert_reduce_fusion.1
  8.6 53.5 %all-gather.8.cloned.1.call-done = bf16[1,4096,256]{2,1,0:T(8,128)(2,1)} async-done(((bf16[1,512,256]{2,1,0:T(8,128)(2,1)}), bf16[1,4096,256]{2,1,0:T(8,128)(2,1)}) %all-gather.8.cloned.1.call-update) | async-done | bytes 2097168 | tf_op jit(solution)/shard_map/all_gather | solution.py:19
  62.2 6.1 %fusion.15 = bf16[768,256]{1,0:T(8,128)(2,1)} fusion(bf16[1,4096,256]{2,1,0:T(8,128)(2,1)} %all-gather.8.cloned.1.call-done, bf16[1,768,4096]{2,1,0:T(8,128)(2,1)} %param.12, s32[1,768,256]{2,1,0:T(8,128)} %param.11, f32[768]{0:T(1024)S(1)} %convert_reduce_fusion.1), kind=kOutput, calls=%fused_computation.13 | convolution fusion | flops 1611399168 | bytes 9571328 | tf_op jit(solution)/shard_map/dot_general | solution.py:20
  68.2 0.0 all-gather.10.cloned.1.call-update
  68.3 0.0 reduce-scatter.3.cloned.1.call-start
  68.3 18.2 %all-gather.10.cloned.1.call-done = bf16[3072,256]{1,0:T(8,128)(2,1)} async-done(((bf16[768,256]{1,0:T(8,128)(2,1)}), bf16[3072,256]{1,0:T(8,128)(2,1)}) %all-gather.10.cloned.1.call-update) | async-done | bytes 1572880 | tf_op jit(solution)/shard_map/all_gather | solution.py:25
  86.6 1.6 broadcast_select_fusion
  88.2 13.7 %convolution_bitcast_fusion = f32[4096,256]{0,1:T(8,128)} fusion(bf16[3072,256]{1,0:T(8,128)(2,1)S(1)} %bitcast.66, bf16[3072,4096]{1,0:T(8,128)(2,1)} %bitcast.64), kind=kOutput, calls=%fused_computation.5 | convolution fusion | flops 6442450944 | bytes 30932992 | tf_op jit(solution)/shard_map/dot_general | solution.py:35
  101.8 0.0 reduce-scatter.3.cloned.1.call-update
  101.8 0.0 all-gather.6.cloned.1.call-start
  101.9 0.9 copy-done.1
  102.8 0.1 copy.11
  102.9 0.0 copy-done.2
  102.9 0.1 convert_reduce_fusion
  103.0 87.4 %reduce-scatter.3.cloned.1.call-done = f32[512,256]{0,1:T(8,128)} async-done(((f32[4096,256]{0,1:T(8,128)}), f32[512,256]{0,1:T(8,128)}) %reduce-scatter.3.cloned.1.call-update) | async-done | bytes 524304 | tf_op jit(solution)/shard_map/reduce_scatter | solution.py:34
  190.5 1.9 multiply_reduce_fusion
  192.4 20.8 %all-reduce = (f32[]{:T(128)}, f32[]{:T(128)}) all-reduce(f32[]{:T(128)} %get-tuple-element.4, f32[]{:T(128)} %get-tuple-element.3), channel_id=1, replica_groups=mesh['layer'=4,'lat'=8] {'lat'}, use_global_device_ids=true, to_apply=%region_3.4 | all-reduce | flops 2 | bytes 16 | tf_op jit(solution)/shard_map/psum | solution.py:45
  213.8 1.9 divide_convert_fusion
  215.7 0.0 all-gather.6.cloned.1.call-update
  215.7 0.0 reduce-scatter.5.cloned.1.call-start
  215.8 48.4 %all-gather.6.cloned.1.call-done = bf16[4096,256]{0,1:T(8,128)(2,1)} async-done(((bf16[512,256]{0,1:T(8,128)(2,1)}), bf16[4096,256]{0,1:T(8,128)(2,1)}) %all-gather.6.cloned.1.call-update) | async-done | bytes 2097168 | tf_op jit(solution)/shard_map/all_gather | solution.py:52
  264.2 13.3 %convolution_bitcast_fusion.1 = f32[3072,256]{0,1:T(8,128)} fusion(bf16[4096,256]{0,1:T(8,128)(2,1)} %all-gather.6.cloned.1.call-done, bf16[3072,4096]{1,0:T(8,128)(2,1)} %bitcast.65), kind=kOutput, calls=%fused_computation.6 | convolution fusion | flops 6442450944 | bytes 30408704 | tf_op jit(solution)/shard_map/dot_general | solution.py:53
  277.5 3.5 %copy.12 = f32[3072,256]{1,0:T(8,128)} copy(f32[3072,256]{0,1:T(8,128)} %convolution_bitcast_fusion.1) | data formatting | bytes 6291456 | tf_op jit(solution)/shard_map/dot_general | solution.py:53
  281.1 3.9 %broadcast_multiply_fusion = f32[4,768,256]{2,1,0:T(8,128)} fusion(f32[4,768,256]{2,1,0:T(8,128)} %bitcast.68, f32[4]{0:T(128)S(1)} %fusion.27), kind=kLoop, calls=%fused_computation.9 | loop fusion | flops 786432 | bytes 6291472 | tf_op jit(solution)/shard_map/mul | solution.py:56
  285.0 0.0 reduce-scatter.5.cloned.1.call-update
  285.7 6.8 %psum.23 = f32[]{:T(128)} all-reduce(f32[]{:T(128)S(6)} %div.23), channel_id=1, replica_groups=mesh['layer'=4,'lat'=8] {'layer'}, use_global_device_ids=true, to_apply=%region_7.8 | all-reduce | flops 1 | bytes 8 | tf_op jit(solution)/shard_map/psum | solution.py:50
  292.5 14.1 %convolution_convert_fusion = bf16[3072,4096]{1,0:T(8,128)(2,1)} fusion(bf16[3072,256]{1,0:T(8,128)(2,1)S(1)} %bitcast.67, bf16[4096,256]{0,1:T(8,128)(2,1)} %all-gather.6.cloned.1.call-done), kind=kOutput, calls=%fused_computation | convolution fusion | flops 6455033856 | bytes 28835840 | tf_op jit(solution)/shard_map/dot_general | solution.py:57
  306.6 14.6 %reduce-scatter.5.cloned.1.call-done = f32[1,768,256]{2,1,0:T(8,128)} async-done(((f32[4,768,256]{2,1,0:T(8,128)}), f32[1,768,256]{2,1,0:T(8,128)}) %reduce-scatter.5.cloned.1.call-update) | async-done | bytes 786448 | tf_op jit(solution)/shard_map/reduce_scatter | solution.py:61
  321.3 6.4 %fusion.2 = bf16[1,768,4096]{2,1,0:T(8,128)(2,1)} fusion(bf16[1,4096,256]{2,1,0:T(8,128)(2,1)} %all-gather.8.cloned.1.call-done, f32[1,768,256]{2,1,0:T(8,128)} %reduce-scatter.5.cloned.1.call-done, s32[1,768,256]{2,1,0:T(8,128)S(1)} %copy-done), kind=kOutput, calls=%fused_computation.4 | convolution fusion | flops 1614348288 | bytes 9961472 | tf_op jit(solution)/shard_map/dot_general | solution.py:63
  (11 shorter events, 0.0 us)
Async XLA Ops:
  7.2 55.0 %all-gather.8.cloned.1.call-start = ((), (), s32[]{:S(2)}) async-start(), calls=%async_computation.5 | async-start | bytes 2359296 | tf_op jit(solution)/shard_map/all_gather | solution.py:19
  7.9 78.7 %all-gather.10.cloned.1.call-start = ((), (), s32[]{:S(2)}) async-start(), calls=%async_computation.6 | async-start | bytes 1966080 | tf_op jit(solution)/shard_map/all_gather | solution.py:25
  68.3 122.2 %reduce-scatter.3.cloned.1.call-start = ((), (), s32[]{:S(2)}) async-start(), calls=%async_computation.2 | async-start | bytes 4718592 | tf_op jit(solution)/shard_map/reduce_scatter | solution.py:34
  101.8 0.9 copy-start.1
  101.8 1.1 copy-start.2
  101.8 1.2 copy-start.3
  101.8 162.3 %all-gather.6.cloned.1.call-start = ((), (), s32[]{:S(2)}) async-start(), calls=%async_computation.3 | async-start | bytes 2359296 | tf_op jit(solution)/shard_map/all_gather | solution.py:52
  215.7 105.6 %reduce-scatter.5.cloned.1.call-start = ((), (), s32[]{:S(2)}) async-start(), calls=%async_computation.4 | async-start | bytes 3932160 | tf_op jit(solution)/shard_map/reduce_scatter | solution.py:61
  292.5 28.8 %copy-start = (s32[1,768,256]{2,1,0:T(8,128)S(1)}, s32[1,768,256]{2,1,0:T(8,128)}, u32[]{:S(2)}) copy-start(s32[1,768,256]{2,1,0:T(8,128)} %param.11) | copy-start | bytes 2359300
Sparse Core Ops, SparseCore 0:
  10.1 51.9 all-gather.7
  68.4 18.1 all-gather.9
  102.0 88.4 reduce-scatter.2
  215.8 48.3 all-gather.5
  285.1 36.1 reduce-scatter.4
where the time goes:
time: 335 us; the launch traced here: 334 us
  waiting for transfers between devices  223 us (67%)
  matrix products  53.6 us (16%)
  blocking collectives  27.6 us (8%)
  between operations  15.2 us (5%)
  other arithmetic  10 us (3%)
  local copies, waits for them, and re-layouts  4.56 us (1%)
    reduce_scatter x1, waiting for transfers between devices, on_device(): lax.psum_scatter(lax.dot_general(weight_rows, stack_rows, (((0,), (0,)),...  87.4 us
    all_gather x1, waiting for transfers between devices, on_device(): whole_inputs = lax.all_gather(inputs_local, 'lat', axis=0, tiled=True)  53.5 us
    all_gather x1, waiting for transfers between devices, on_device(): full_grad = lax.all_gather(out_grad, 'lat', axis=0, tiled=True)  48.4 us
    psum x1, blocking collectives, on_device(): lax.psum((jnp.sum(residual_err * residual_err), jnp.sum(centered * center...  20.8 us
    all_gather x1, waiting for transfers between devices, on_device(): gathered = lax.all_gather(latents[None], 'layer', axis=0, tiled=True)  18.2 us
    reduce_scatter x1, waiting for transfers between devices, on_device(): lax.psum_scatter(grad_rows, 'layer', scatter_dimension=0, tiled=True)[0]  14.6 us
    dot_general x1, matrix products, on_device(): lax.dot_general(stack_rows, full_grad, (((1,), (1,)), ((), ())), preferre...  14.1 us
    dot_general x1, matrix products, on_device(): lax.dot_general(weight_rows, stack_rows, (((0,), (0,)), ((), ())), prefer...  13.7 us
  transfers between devices with their start and end apart: 5, of which 5 were waited for; matrix products, arithmetic and copies ran while one was open for 5% of the time, Pallas kernels for 0%

commit v1 on v0

--- a/solution.py
+++ b/solution.py
@@ -16,7 +16,12 @@
     lat_rows = weight_enc.shape[0]
     feature_count = weight_enc.shape[1]
     token_count = inputs_local.shape[1]
-    whole_inputs = lax.all_gather(inputs_local, "lat", axis=0, tiled=True)
+    ring = [inputs_local]
+    for hop in range(7):
+        ring.append(lax.ppermute(ring[-1], "lat", [(dev, (dev + 1) % 8) for dev in range(8)]))
+    whole_inputs = jnp.roll(
+        jnp.concatenate(ring[::-1], axis=0), (lax.axis_index("lat") + 1) * ring[0].shape[0], axis=0
+    )
     preact = jnp.dot(weight_enc, whole_inputs, preferred_element_type=jnp.float32)
     preact = preact + enc_bias[0].astype(jnp.float32)[:, None]
     gating = active_mask[0].astype(jnp.float32)

time: 335 us -> 349 us (1.042)
  local copies, waits for them, and re-layouts: 4.56 us -> 14.1 us
  waiting for transfers between devices: 223 us -> 231 us
  matrix products: 53.6 us -> 49.1 us
    ppermute x0 -> x7, waiting for transfers between devices: none -> 63.7 us  [on_device(): lax.ppermute(ring[-1], 'lat', [(dev, (dev + 1) % 8) for dev in range(8)])]
    all_gather x1 -> x0, waiting for transfers between devices: 53.5 us -> none  [on_device(): whole_inputs = lax.all_gather(inputs_local, 'lat', axis=0, tiled=True)]
    unnamed x9 -> x38, local copies, waits for them, and re-layouts: 1.02 us -> 6.09 us
  transfers between devices with their start and end apart: 5 -> 11, of which waited for: 5 -> 11; matrix products, arithmetic and copies ran while one was open for 5% -> 5% of each run, Pallas kernels for 0% -> 0%
where the time goes in v1:
time: 349 us; the launch traced here: 348 us
  waiting for transfers between devices  231 us (66%)
  matrix products  49.1 us (14%)
  blocking collectives  27.5 us (8%)
  between operations  15.5 us (4%)
  local copies, waits for them, and re-layouts  14.1 us (4%)
  other arithmetic  7.31 us (2%)
    reduce_scatter x1, waiting for transfers between devices, on_device(): lax.psum_scatter(lax.dot_general(weight_rows, stack_rows, (((0,), (0,)),...  87.5 us
    ppermute x7, waiting for transfers between devices, on_device(): lax.ppermute(ring[-1], 'lat', [(dev, (dev + 1) % 8) for dev in range(8)])  63.7 us
    all_gather x1, waiting for transfers between devices, on_device(): full_grad = lax.all_gather(out_grad, 'lat', axis=0, tiled=True)  48.2 us
    psum x1, blocking collectives, on_device(): lax.psum((jnp.sum(residual_err * residual_err), jnp.sum(centered * center...  20.8 us
    all_gather x1, waiting for transfers between devices, on_device(): gathered = lax.all_gather(latents[None], 'layer', axis=0, tiled=True)  17.1 us
    reduce_scatter x1, waiting for transfers between devices, on_device(): lax.psum_scatter(grad_rows, 'layer', scatter_dimension=0, tiled=True)[0]  14.7 us
    dot_general x1, matrix products, on_device(): lax.dot_general(stack_rows, full_grad, (((1,), (1,)), ((), ())), preferre...  14.2 us
    dot_general x1, matrix products, on_device(): lax.dot_general(weight_rows, stack_rows, (((0,), (0,)), ((), ())), prefer...  13.6 us
  transfers between devices with their start and end apart: 11, of which 11 were waited for; matrix products, arithmetic and copies ran while one was open for 5% of the time, Pallas kernels for 0%

profile of v1, /device:TPU:0, one launch (start us, length us, event | category | flops | bytes accessed | tf_op | source)
XLA Modules:
  0.0 348.0 jit_solution(655161006146315568)
XLA Ops:
  7.2 3.0 collective-permute-start
  10.2 9.6 %collective-permute-done = bf16[512,256]{1,0:T(8,128)(2,1)S(1)} collective-permute-done((bf16[512,256]{1,0:T(8,128)(2,1)}, bf16[512,256]{1,0:T(8,128)(2,1)S(1)}, u32[]{:S(2)}, u32[]{:S(2)}) %collective-permute-start) | collective-permute-done | bytes 262176 | tf_op jit(solution)/shard_map/ppermute | solution.py:21
  19.8 10.2 %collective-permute-done.1 = bf16[512,256]{1,0:T(8,128)(2,1)S(1)} collective-permute-done((bf16[512,256]{1,0:T(8,128)(2,1)S(1)}, bf16[512,256]{1,0:T(8,128)(2,1)S(1)}, u32[]{:S(2)}, u32[]{:S(2)}) %collective-permute-start.1) | collective-permute-done | bytes 262176 | tf_op jit(solution)/shard_map/ppermute | solution.py:21
  30.0 9.3 %collective-permute-done.2 = bf16[512,256]{1,0:T(8,128)(2,1)S(1)} collective-permute-done((bf16[512,256]{1,0:T(8,128)(2,1)S(1)}, bf16[512,256]{1,0:T(8,128)(2,1)S(1)}, u32[]{:S(2)}, u32[]{:S(2)}) %collective-permute-start.2) | collective-permute-done | bytes 262176 | tf_op jit(solution)/shard_map/ppermute | solution.py:21
  39.3 9.1 %collective-permute-done.3 = bf16[512,256]{1,0:T(8,128)(2,1)S(1)} collective-permute-done((bf16[512,256]{1,0:T(8,128)(2,1)S(1)}, bf16[512,256]{1,0:T(8,128)(2,1)S(1)}, u32[]{:S(2)}, u32[]{:S(2)}) %collective-permute-start.3) | collective-permute-done | bytes 262176 | tf_op jit(solution)/shard_map/ppermute | solution.py:21
  48.3 9.1 %collective-permute-done.4 = bf16[512,256]{1,0:T(8,128)(2,1)S(1)} collective-permute-done((bf16[512,256]{1,0:T(8,128)(2,1)S(1)}, bf16[512,256]{1,0:T(8,128)(2,1)S(1)}, u32[]{:S(2)}, u32[]{:S(2)}) %collective-permute-start.4) | collective-permute-done | bytes 262176 | tf_op jit(solution)/shard_map/ppermute | solution.py:21
  57.4 9.7 %collective-permute-done.5 = bf16[512,256]{1,0:T(8,128)(2,1)S(1)} collective-permute-done((bf16[512,256]{1,0:T(8,128)(2,1)S(1)}, bf16[512,256]{1,0:T(8,128)(2,1)S(1)}, u32[]{:S(2)}, u32[]{:S(2)}) %collective-permute-start.5) | collective-permute-done | bytes 262176 | tf_op jit(solution)/shard_map/ppermute | solution.py:21
  67.1 1.4 copy.13
  68.5 0.7 convert_reduce_fusion.1
  69.3 6.9 %collective-permute-done.6 = bf16[512,256]{1,0:T(8,128)(2,1)S(1)} collective-permute-done((bf16[512,256]{1,0:T(8,128)(2,1)S(1)}, bf16[512,256]{1,0:T(8,128)(2,1)S(1)}, u32[]{:S(2)}, u32[]{:S(2)}) %collective-permute-start.6) | collective-permute-done | bytes 262176 | tf_op jit(solution)/shard_map/ppermute | solution.py:21
  76.6 1.9 copy-done.4
  78.6 2.6 fusion.20
  81.3 17.1 %all-gather.6.cloned.1.call-done = bf16[3072,256]{0,1:T(8,128)(2,1)} async-done(((bf16[768,256]{0,1:T(8,128)(2,1)}), bf16[3072,256]{0,1:T(8,128)(2,1)}) %all-gather.6.cloned.1.call-update) | async-done | bytes 1572880 | tf_op jit(solution)/shard_map/all_gather | solution.py:30
  98.4 3.3 reshape.48
  101.7 0.7 broadcast_select_fusion
  102.4 0.3 copy.17
  102.7 1.1 copy-done
  103.8 13.6 %convolution_bitcast_fusion = f32[4096,256]{0,1:T(8,128)} fusion(bf16[3072,256]{0,1:T(8,128)(2,1)S(1)} %bitcast.69, bf16[3072,4096]{1,0:T(8,128)(2,1)} %bitcast.75), kind=kOutput, calls=%fused_computation.5 | convolution fusion | flops 6442450944 | bytes 30932992 | tf_op jit(solution)/shard_map/dot_general | solution.py:40
  117.5 0.6 copy-done.7
  118.6 87.5 %reduce-scatter.3.cloned.1.call-done = f32[512,256]{0,1:T(8,128)} async-done(((f32[4096,256]{0,1:T(8,128)}), f32[512,256]{0,1:T(8,128)}) %reduce-scatter.3.cloned.1.call-update) | async-done | bytes 524304 | tf_op jit(solution)/shard_map/reduce_scatter | solution.py:39
  206.1 1.9 multiply_reduce_fusion
  208.0 20.8 %all-reduce = (f32[]{:T(128)}, f32[]{:T(128)}) all-reduce(f32[]{:T(128)} %get-tuple-element.4, f32[]{:T(128)} %get-tuple-element.3), channel_id=1, replica_groups=mesh['layer'=4,'lat'=8] {'lat'}, use_global_device_ids=true, to_apply=%region_3.4 | all-reduce | flops 2 | bytes 16 | tf_op jit(solution)/shard_map/psum | solution.py:50
  229.5 1.9 divide_convert_fusion
  231.6 48.2 %all-gather.4.cloned.1.call-done = bf16[4096,256]{0,1:T(8,128)(2,1)} async-done(((bf16[512,256]{0,1:T(8,128)(2,1)}), bf16[4096,256]{0,1:T(8,128)(2,1)}) %all-gather.4.cloned.1.call-update) | async-done | bytes 2097168 | tf_op jit(solution)/shard_map/all_gather | solution.py:57
  279.8 12.2 %convolution_bitcast_fusion.1 = f32[3072,256]{0,1:T(8,128)S(1)} fusion(bf16[4096,256]{0,1:T(8,128)(2,1)} %all-gather.4.cloned.1.call-done, bf16[3072,4096]{1,0:T(8,128)(2,1)} %bitcast.76), kind=kOutput, calls=%fused_computation.6 | convolution fusion | flops 6442450944 | bytes 30408704 | tf_op jit(solution)/shard_map/dot_general | solution.py:58
  292.0 2.4 copy.15
  294.4 2.4 copy.16
  296.8 2.0 broadcast_multiply_fusion
  299.6 6.7 %psum.23 = f32[]{:T(128)} all-reduce(f32[]{:T(128)S(6)} %div.23), channel_id=1, replica_groups=mesh['layer'=4,'lat'=8] {'layer'}, use_global_device_ids=true, to_apply=%region_7.8 | all-reduce | flops 1 | bytes 8 | tf_op jit(solution)/shard_map/psum | solution.py:55
  306.2 14.2 %convolution_convert_fusion = bf16[3072,4096]{1,0:T(8,128)(2,1)} fusion(bf16[3072,256]{0,1:T(8,128)(2,1)S(1)} %bitcast.70, bf16[4096,256]{0,1:T(8,128)(2,1)} %all-gather.4.cloned.1.call-done), kind=kOutput, calls=%fused_computation | convolution fusion | flops 6455033856 | bytes 28835840 | tf_op jit(solution)/shard_map/dot_general | solution.py:62
  320.4 14.7 %reduce-scatter.5.cloned.1.call-done = f32[1,768,256]{1,2,0:T(8,128)} async-done(((f32[4,768,256]{1,2,0:T(8,128)}), f32[1,768,256]{1,2,0:T(8,128)}) %reduce-scatter.5.cloned.1.call-update) | async-done | bytes 786448 | tf_op jit(solution)/shard_map/reduce_scatter | solution.py:66
  335.1 6.4 %fusion.2 = bf16[1,768,4096]{2,1,0:T(8,128)(2,1)} fusion(bf16[8192,256]{1,0:T(8,128)(2,1)} %copy-done.4, s32[]{:T(128)S(6)} %select_n.18, f32[1,768,256]{1,2,0:T(8,128)} %reduce-scatter.5.cloned.1.call-done, s32[1,768,256]{1,2,0:T(8,128)S(1)} %copy-done.3), kind=kOutput, calls=%fused_computation.4 | convolution fusion | flops 1614348288 | bytes 9961476 | tf_op jit(solution)/shard_map/dot_general | solution.py:68
  (54 shorter events, 1.3 us)
Async XLA Ops:
  7.2 69.2 %copy-start.5 = (bf16[1,512,256]{2,1,0:T(8,128)(2,1)S(1)}, bf16[1,512,256]{2,1,0:T(8,128)(2,1)}, u32[]{:S(2)}) copy-start(bf16[1,512,256]{2,1,0:T(8,128)(2,1)} %param.8) | copy-start | bytes 786436
  7.2 91.2 %all-gather.6.cloned.1.call-start = ((), (), s32[]{:S(2)}) async-start(), calls=%async_computation.5 | async-start | bytes 1966080 | tf_op jit(solution)/shard_map/all_gather | solution.py:30
  7.2 12.6 %collective-permute-start = (bf16[512,256]{1,0:T(8,128)(2,1)}, bf16[512,256]{1,0:T(8,128)(2,1)S(1)}, u32[]{:S(2)}, u32[]{:S(2)}) collective-permute-start(bf16[512,256]{1,0:T(8,128)(2,1)} %bitcast.72), channel_id=1, source_target_pairs={{0,1},{1,2},{2,3},{3,4},{4,5},{5,6},{6,7},{7,0},{8,9},{9,10},{10,1... | collective-permute-start | bytes 786440 | tf_op jit(solution)/shard_map/ppermute | solution.py:21
  19.8 10.2 %collective-permute-start.1 = (bf16[512,256]{1,0:T(8,128)(2,1)S(1)}, bf16[512,256]{1,0:T(8,128)(2,1)S(1)}, u32[]{:S(2)}, u32[]{:S(2)}) collective-permute-start(bf16[512,256]{1,0:T(8,128)(2,1)S(1)} %collective-permute-done), channel_id=1, source_target_pairs={{0,1},{1,2},{2,3},{3,4},{4,5},{5,6},{6,7},{7,0},{8,9},{9,10},{10,1... | collective-permute-start | bytes 786440 | tf_op jit(solution)/shard_map/ppermute | solution.py:21
  30.0 9.3 %collective-permute-start.2 = (bf16[512,256]{1,0:T(8,128)(2,1)S(1)}, bf16[512,256]{1,0:T(8,128)(2,1)S(1)}, u32[]{:S(2)}, u32[]{:S(2)}) collective-permute-start(bf16[512,256]{1,0:T(8,128)(2,1)S(1)} %collective-permute-done.1), channel_id=1, source_target_pairs={{0,1},{1,2},{2,3},{3,4},{4,5},{5,6},{6,7},{7,0},{8,9},{9,10},{10,1... | collective-permute-start | bytes 786440 | tf_op jit(solution)/shard_map/ppermute | solution.py:21
  39.3 9.1 %collective-permute-start.3 = (bf16[512,256]{1,0:T(8,128)(2,1)S(1)}, bf16[512,256]{1,0:T(8,128)(2,1)S(1)}, u32[]{:S(2)}, u32[]{:S(2)}) collective-permute-start(bf16[512,256]{1,0:T(8,128)(2,1)S(1)} %collective-permute-done.2), channel_id=1, source_target_pairs={{0,1},{1,2},{2,3},{3,4},{4,5},{5,6},{6,7},{7,0},{8,9},{9,10},{10,1... | collective-permute-start | bytes 786440 | tf_op jit(solution)/shard_map/ppermute | solution.py:21
  48.3 9.1 %collective-permute-start.4 = (bf16[512,256]{1,0:T(8,128)(2,1)S(1)}, bf16[512,256]{1,0:T(8,128)(2,1)S(1)}, u32[]{:S(2)}, u32[]{:S(2)}) collective-permute-start(bf16[512,256]{1,0:T(8,128)(2,1)S(1)} %collective-permute-done.3), channel_id=1, source_target_pairs={{0,1},{1,2},{2,3},{3,4},{4,5},{5,6},{6,7},{7,0},{8,9},{9,10},{10,1... | collective-permute-start | bytes 786440 | tf_op jit(solution)/shard_map/ppermute | solution.py:21
  57.4 9.7 %collective-permute-start.5 = (bf16[512,256]{1,0:T(8,128)(2,1)S(1)}, bf16[512,256]{1,0:T(8,128)(2,1)S(1)}, u32[]{:S(2)}, u32[]{:S(2)}) collective-permute-start(bf16[512,256]{1,0:T(8,128)(2,1)S(1)} %collective-permute-done.4), channel_id=1, source_target_pairs={{0,1},{1,2},{2,3},{3,4},{4,5},{5,6},{6,7},{7,0},{8,9},{9,10},{10,1... | collective-permute-start | bytes 786440 | tf_op jit(solution)/shard_map/ppermute | solution.py:21
  67.1 9.1 %collective-permute-start.6 = (bf16[512,256]{1,0:T(8,128)(2,1)S(1)}, bf16[512,256]{1,0:T(8,128)(2,1)S(1)}, u32[]{:S(2)}, u32[]{:S(2)}) collective-permute-start(bf16[512,256]{1,0:T(8,128)(2,1)S(1)} %collective-permute-done.5), channel_id=1, source_target_pairs={{0,1},{1,2},{2,3},{3,4},{4,5},{5,6},{6,7},{7,0},{8,9},{9,10},{10,1... | collective-permute-start | bytes 786440 | tf_op jit(solution)/shard_map/ppermute | solution.py:21
  68.5 8.1 %copy-start.2 = (s32[1,768,256]{1,2,0:T(8,128)}, s32[1,768,256]{1,2,0:T(8,128)S(1)}, u32[]{:S(2)}) copy-start(s32[1,768,256]{1,2,0:T(8,128)S(1)} %copy.13) | copy-start | bytes 2359300
  69.3 9.3 %copy-start.9 = (bf16[1,768,4096]{2,1,0:T(8,128)(2,1)S(1)}, bf16[1,768,4096]{2,1,0:T(8,128)(2,1)}, u32[]{:S(2)}) copy-start(bf16[1,768,4096]{2,1,0:T(8,128)(2,1)} %param.12) | copy-start | bytes 18874372
  76.6 1.9 copy-start.4
  81.3 124.8 %reduce-scatter.3.cloned.1.call-start = ((), (), s32[]{:S(2)}) async-start(), calls=%async_computation.2 | async-start | bytes 4718592 | tf_op jit(solution)/shard_map/reduce_scatter | solution.py:39
  102.7 1.1 copy-start
  117.4 0.7 copy-start.7
  117.4 1.0 copy-start.6
  117.4 1.2 copy-start.8
  117.5 162.3 %all-gather.4.cloned.1.call-start = ((), (), s32[]{:S(2)}) async-start(), calls=%async_computation.3 | async-start | bytes 2359296 | tf_op jit(solution)/shard_map/all_gather | solution.py:57
  231.3 103.7 %reduce-scatter.5.cloned.1.call-start = ((), (), s32[]{:S(2)}) async-start(), calls=%async_computation.4 | async-start | bytes 3932160 | tf_op jit(solution)/shard_map/reduce_scatter | solution.py:66
  298.8 7.5 %copy-start.1 = (bf16[32,8,4,768]{3,1,2,0:T(8,128)(2,1)S(1)}, bf16[32,8,4,768]{3,1,2,0:T(8,128)(2,1)}, u32[]{:S(2)}) copy-start(bf16[32,8,4,768]{3,1,2,0:T(8,128)(2,1)} %copy-done) | copy-start | bytes 4718596
  306.2 28.9 %copy-start.3 = (s32[1,768,256]{1,2,0:T(8,128)S(1)}, s32[1,768,256]{1,2,0:T(8,128)}, u32[]{:S(2)}) copy-start(s32[1,768,256]{1,2,0:T(8,128)} %copy-done.2) | copy-start | bytes 2359300
Sparse Core Ops, SparseCore 0:
  81.4 16.9 all-gather.5
  117.6 88.4 reduce-scatter.2
  231.5 48.2 all-gather.3
  298.9 36.1 reduce-scatter.4
